TPU v7x, 32 devices: a whole 2x2x4 slice. The times are simulated.
32 devices in a mesh: row: 16 (over z, y, x), col: 2 (over core).
Axes of the slice: x: 2, y: 2, z: 4, core: 2. Of those that a mesh axis runs over, the one named last changes fastest.
Arguments:
- latent: bfloat16 [6144, 512], P('row', 'col'), may hold values from -6 to 6
- w_kv: bfloat16 [512, 8192], P('row', 'col'), may hold values from -0.25 to 0.25
- queries: bfloat16 [6144, 4096], P('row', 'col'), may hold values from -240 to 240
- w_out: bfloat16 [4096, 7168], P('row', 'col'), may hold values from -0.09375 to 0.09375
Outputs:
- mixed: bfloat16 [6144, 7168], P('row', 'col')
All inputs are finite; a program needn't handle non-finite values.
Results may differ from a plain program's by a relative error of at most 0.012.
The roundings to bfloat16 on the way count: a program that leaves them out, or rounds other values in their place, can miss the bound.
Values may be sent and summed in bfloat16 or wider, within the bound.
No kernel may reach another device: no remote copies, remote signals or barrier semaphores. Data moves between devices by JAX's collectives and lax.ppermute only.
A program may use at most 128 MiB of HBM per device.

v0:
```python
import math
import jax
import jax.numpy as jnp
from jax import lax
from jax.sharding import PartitionSpec as P

HEAD = 128
NEG_FILL = -1e30


def per_device(latent, w_kv, queries, w_out):
    row_count = lax.axis_size("row")
    tok_rows = latent.shape[0]
    per_col = queries.shape[1] // HEAD
    quarters = row_count // per_col
    stripe = tok_rows // quarters
    my_row = lax.axis_index("row")
    quarter = my_row // per_col
    pair_width = 2 * HEAD
    latent_rows = lax.all_gather(latent, "col", axis=1, tiled=True)
    columns = latent_rows
    summed = jnp.dot(
        columns, lax.all_gather(w_kv, "row", axis=0, tiled=True), preferred_element_type=jnp.float32
    )
    expanded = summed.astype(jnp.bfloat16).reshape(tok_rows, per_col, pair_width).transpose(1, 0, 2)
    copies = jnp.broadcast_to(expanded[None], (quarters, per_col, tok_rows, pair_width))
    copies = copies.reshape(row_count, tok_rows, pair_width)
    keyvals = lax.all_to_all(copies, "row", split_axis=0, concat_axis=1, tiled=True).reshape(
        row_count * tok_rows, pair_width
    )
    split_queries = queries.reshape(quarters, stripe, per_col, HEAD).transpose(0, 2, 1, 3)
    split_queries = split_queries.reshape(row_count, stripe, HEAD)
    my_queries = lax.all_to_all(
        split_queries, "row", split_axis=0, concat_axis=1, tiled=True
    ).reshape(row_count * stripe, HEAD)
    sources_per_block = row_count
    for candidate in range(1, row_count + 1):
        if row_count % candidate == 0 and candidate * stripe >= 256:
            sources_per_block = candidate
            break
    block_rows = sources_per_block * stripe
    key_span = sources_per_block * tok_rows
    key_block = math.gcd(key_span, 512)
    score_scale = HEAD ** (-0.5)
    pieces_done = []
    for block_index in range(row_count // sources_per_block):
        query_block = my_queries[block_index * block_rows : (block_index + 1) * block_rows]
        local_rows = jnp.arange(block_rows, dtype=jnp.int32)
        query_pos = (
            (block_index * sources_per_block + local_rows // stripe) * tok_rows
            + quarter * stripe
            + local_rows % stripe
        )

        def key_turn(key_index, carry, query_block=query_block, query_pos=query_pos):
            running_max, running_sum, weighted = carry
            first_key = key_index * key_block
            pairs = lax.dynamic_slice_in_dim(keyvals, first_key, key_block, 0)
            scores = (
                lax.dot_general(
                    query_block,
                    pairs[:, :HEAD],
                    (((1,), (1,)), ((), ())),
                    preferred_element_type=jnp.float32,
                )
                * score_scale
            )
            key_pos = first_key + jnp.arange(key_block, dtype=jnp.int32)
            allowed = key_pos[None, :] <= query_pos[:, None]
            scores = jnp.where(allowed, scores, NEG_FILL)
            new_max = jnp.maximum(running_max, jnp.max(scores, axis=1))
            rescale = jnp.exp(running_max - new_max)
            weights = jnp.where(allowed, jnp.exp(scores - new_max[:, None]), 0.0)
            running_sum = running_sum * rescale + jnp.sum(weights, axis=1)
            weighted = weighted * rescale[:, None] + jnp.dot(
                weights.astype(jnp.bfloat16), pairs[:, HEAD:], preferred_element_type=jnp.float32
            )
            return (new_max, running_sum, weighted)

        starting = (
            jnp.full((block_rows,), NEG_FILL, jnp.float32),
            jnp.zeros((block_rows,), jnp.float32),
            jnp.zeros((block_rows, HEAD), jnp.float32),
        )
        last_pos = (
            ((block_index + 1) * sources_per_block - 1) * tok_rows + quarter * stripe + stripe - 1
        )
        key_steps = (last_pos + key_block) // key_block
        final_max, final_sum, final_weighted = lax.fori_loop(0, key_steps, key_turn, starting)
        pieces_done.append((final_weighted / final_sum[:, None]).astype(jnp.bfloat16))
    attended = jnp.concatenate(pieces_done, axis=0)
    returned = lax.all_to_all(
        attended.reshape(row_count, stripe, HEAD), "row", split_axis=0, concat_axis=0, tiled=True
    )
    attn_tokens = (
        returned.reshape(quarters, per_col, stripe, HEAD)
        .transpose(0, 2, 1, 3)
        .reshape(tok_rows, per_col * HEAD)
    )
    full_features = lax.all_gather(attn_tokens, "col", axis=1, tiled=True)
    columns = full_features
    mixed = jnp.dot(
        columns,
        lax.all_gather(w_out, "row", axis=0, tiled=True),
        preferred_element_type=jnp.float32,
    )
    return mixed.astype(jnp.bfloat16)


def solution(mesh):
    in_specs = (P("row", "col"), P("row", "col"), P("row", "col"), P("row", "col"))
    out_specs = P("row", "col")
    return jax.shard_map(
        per_device, mesh=mesh, in_specs=in_specs, out_specs=out_specs, check_vma=False
    )
```

profile of v0, /device:TPU:0, one launch (start us, length us, event | category | flops | bytes accessed | tf_op | source)
XLA Modules:
  0.0 2180.4 jit_solution(16351844525132143396)
XLA Ops:
  7.3 2.6 copy.44
  9.9 8.3 all-to-all-start.1
  18.2 2.1 all_gather.12
  20.3 83.3 %all-gather.4.cloned.1.call-done = bf16[512,4096]{1,0:T(8,128)(2,1)} async-done(((bf16[32,4096]{1,0:T(8,128)(2,1)}), bf16[512,4096]{1,0:T(8,128)(2,1)}) %all-gather.4.cloned.1.call-update) | async-done | bytes 4194320 | tf_op jit(solution)/shard_map/all_gather | solution.py:23
  103.6 4.0 convolution_convert_fusion.1
  107.6 2.0 copy.64
  110.7 4.2 all-to-all-start
  115.5 2.5 slice_bitcast_fusion
  140.6 35.0 %all-to-all-done = bf16[16,384,256]{2,1,0:T(8,128)(2,1)S(1)} async-done(((bf16[16,384,256]{2,1,0:T(8,128)(2,1)}), bf16[16,384,256]{2,1,0:T(8,128)(2,1)S(1)}, u32[]{:S(2)}, u32[]{:S(2)}) %all-to-all-start) | async-done | bytes 3145760 | tf_op jit(solution)/shard_map/all_to_all | solution.py:28
  176.2 10.4 while.240
  188.0 26.5 %while.241 = (s32[]{:T(128)}, f32[384]{0:T(512)S(1)}, f32[384]{0:T(512)}, f32[384,128]{1,0:T(8,128)}, s32[]{:T(128)}, /*index=5*/bf16[6144,256]{1,0:T(8,128)(2,1...) while((s32[]{:T(128)}, f32[384]{0:T(512)S(1)}, ...), condition=%wide.region_7.8_spmd.clone, body=%wide.region_4.7_spmd.clone.sunk | while | flops 25859080 | bytes 1183975 | solution.py:89
  215.1 31.5 %while.242 = (s32[]{:T(128)}, f32[384]{0:T(512)S(1)}, f32[384]{0:T(512)}, f32[384,128]{1,0:T(8,128)S(1)}, s32[]{:T(128)}, /*index=5*/bf16[6144,256]{1,0:T(8,128)...) while((s32[]{:T(128)}, f32[384]{0:T(512)S(1)}, ...), condition=%wide.region_11.12_spmd.clone, body=%wide.region_8.11_spmd.clone.sunk | while | flops 25859080 | bytes 1183975 | solution.py:89
  247.9 53.3 %while.243 = (s32[]{:T(128)}, f32[384]{0:T(512)S(1)}, f32[384]{0:T(512)}, f32[384,128]{1,0:T(8,128)}, s32[]{:T(128)}, /*index=5*/bf16[6144,256]{1,0:T(8,128)(2,1...) while((s32[]{:T(128)}, f32[384]{0:T(512)S(1)}, ...), condition=%wide.region_15.16_spmd.clone, body=%wide.region_12.15_spmd.clone.sunk | while | flops 25859080 | bytes 1183975 | solution.py:89
  250.5 1.9 convolution_add_fusion.35
  254.9 1.9 convolution_add_fusion.35
  259.3 1.9 convolution_add_fusion.35
  263.8 1.9 convolution_add_fusion.35
  268.2 1.9 convolution_add_fusion.35
  272.7 1.9 convolution_add_fusion.35
  277.1 1.9 convolution_add_fusion.35
  281.5 1.9 convolution_add_fusion.35
  286.0 1.9 convolution_add_fusion.35
  290.4 1.9 convolution_add_fusion.35
  294.9 1.9 convolution_add_fusion.35
  299.3 1.9 convolution_add_fusion.35
  301.8 50.9 %while.244 = (s32[]{:T(128)}, f32[384]{0:T(512)S(1)}, f32[384]{0:T(512)}, f32[384,128]{1,0:T(8,128)S(1)}, s32[]{:T(128)}, /*index=5*/bf16[6144,256]{1,0:T(8,128)...) while((s32[]{:T(128)}, f32[384]{0:T(512)S(1)}, ...), condition=%wide.region_19.20_spmd.clone, body=%wide.region_16.19_spmd.clone.sunk | while | flops 25859080 | bytes 1183975 | solution.py:89
  354.0 79.4 %while.245 = (s32[]{:T(128)}, f32[384]{0:T(512)S(1)}, f32[384]{0:T(512)}, f32[384,128]{1,0:T(8,128)}, s32[]{:T(128)}, /*index=5*/bf16[6144,256]{1,0:T(8,128)(2,1...) while((s32[]{:T(128)}, f32[384]{0:T(512)S(1)}, ...), condition=%wide.region_23.24_spmd.clone, body=%wide.region_20.23_spmd.clone.sunk | while | flops 25859080 | bytes 1183975 | solution.py:89
  434.1 71.6 %while.246 = (s32[]{:T(128)}, f32[384]{0:T(512)S(1)}, f32[384]{0:T(512)}, f32[384,128]{1,0:T(8,128)S(1)}, s32[]{:T(128)}, /*index=5*/bf16[6144,256]{1,0:T(8,128)...) while((s32[]{:T(128)}, f32[384]{0:T(512)S(1)}, ...), condition=%wide.region_27.28_spmd.clone, body=%wide.region_24.27_spmd.clone.sunk | while | flops 25859080 | bytes 1183975 | solution.py:89
  507.1 106.1 %while.247 = (s32[]{:T(128)}, f32[384]{0:T(512)S(1)}, f32[384]{0:T(512)}, f32[384,128]{1,0:T(8,128)}, s32[]{:T(128)}, /*index=5*/bf16[6144,256]{1,0:T(8,128)(2,1...) while((s32[]{:T(128)}, f32[384]{0:T(512)S(1)}, ...), condition=%wide.region_31.32_spmd.clone, body=%wide.region_28.31_spmd.clone.sunk | while | flops 25859080 | bytes 1183975 | solution.py:89
  509.6 1.9 convolution_add_fusion.39
  514.0 1.9 convolution_add_fusion.39
  518.4 1.9 convolution_add_fusion.39
  522.8 1.9 convolution_add_fusion.39
  527.3 1.9 convolution_add_fusion.39
  531.7 1.9 convolution_add_fusion.39
  536.1 1.9 convolution_add_fusion.39
  540.5 1.9 convolution_add_fusion.39
  544.9 1.9 convolution_add_fusion.39
  549.4 1.9 convolution_add_fusion.39
  553.8 1.9 convolution_add_fusion.39
  558.2 1.9 convolution_add_fusion.39
  562.6 1.9 convolution_add_fusion.39
  567.0 1.9 convolution_add_fusion.39
  571.5 1.9 convolution_add_fusion.39
  575.9 1.9 convolution_add_fusion.39
  580.3 1.9 convolution_add_fusion.39
  584.7 1.9 convolution_add_fusion.39
  589.1 1.9 convolution_add_fusion.39
  593.6 1.9 convolution_add_fusion.39
  598.0 1.9 convolution_add_fusion.39
  602.4 1.9 convolution_add_fusion.39
  606.8 1.9 convolution_add_fusion.39
  613.8 94.2 %while.248 = (s32[]{:T(128)}, f32[384]{0:T(512)S(1)}, f32[384]{0:T(512)}, f32[384,128]{1,0:T(8,128)S(1)}, s32[]{:T(128)}, /*index=5*/bf16[6144,256]{1,0:T(8,128)...) while((s32[]{:T(128)}, f32[384]{0:T(512)S(1)}, ...), condition=%wide.region_35.36_spmd.clone, body=%wide.region_32.35_spmd.clone.sunk | while | flops 25859080 | bytes 1183975 | solution.py:89
  709.4 132.6 %while.249 = (s32[]{:T(128)}, f32[384]{0:T(512)S(1)}, f32[384]{0:T(512)}, f32[384,128]{1,0:T(8,128)}, s32[]{:T(128)}, /*index=5*/bf16[6144,256]{1,0:T(8,128)(2,1...) while((s32[]{:T(128)}, f32[384]{0:T(512)S(1)}, ...), condition=%wide.region_39.40_spmd.clone, body=%wide.region_36.39_spmd.clone.sunk | while | flops 25859080 | bytes 1183975 | solution.py:89
  842.6 116.8 %while.250 = (s32[]{:T(128)}, f32[384]{0:T(512)S(1)}, f32[384]{0:T(512)}, f32[384,128]{1,0:T(8,128)S(1)}, s32[]{:T(128)}, /*index=5*/bf16[6144,256]{1,0:T(8,128)...) while((s32[]{:T(128)}, f32[384]{0:T(512)S(1)}, ...), condition=%wide.region_43.44_spmd.clone, body=%wide.region_40.43_spmd.clone.sunk | while | flops 25859080 | bytes 1183975 | solution.py:89
  960.8 158.0 %while.251 = (s32[]{:T(128)}, f32[384]{0:T(512)S(1)}, f32[384]{0:T(512)}, f32[384,128]{1,0:T(8,128)}, s32[]{:T(128)}, /*index=5*/bf16[6144,256]{1,0:T(8,128)(2,1...) while((s32[]{:T(128)}, f32[384]{0:T(512)S(1)}, ...), condition=%wide.region_47.48_spmd.clone, body=%wide.region_44.47_spmd.clone.sunk | while | flops 25859080 | bytes 1183975 | solution.py:89
  1119.4 134.8 %while.252 = (s32[]{:T(128)}, f32[384]{0:T(512)S(1)}, f32[384]{0:T(512)}, f32[384,128]{1,0:T(8,128)S(1)}, s32[]{:T(128)}, /*index=5*/bf16[6144,256]{1,0:T(8,128)...) while((s32[]{:T(128)}, f32[384]{0:T(512)S(1)}, ...), condition=%wide.region_51.52_spmd.clone, body=%wide.region_48.51_spmd.clone.sunk | while | flops 25859080 | bytes 1183975 | solution.py:89
  1255.5 185.7 %while.253 = (s32[]{:T(128)}, f32[384]{0:T(512)S(1)}, f32[384]{0:T(512)}, f32[384,128]{1,0:T(8,128)}, s32[]{:T(128)}, /*index=5*/bf16[6144,256]{1,0:T(8,128)(2,1...) while((s32[]{:T(128)}, f32[384]{0:T(512)S(1)}, ...), condition=%wide.region_55.56_spmd.clone, body=%wide.region_52.55_spmd.clone.sunk | while | flops 25859080 | bytes 1183975 | solution.py:89
  1441.8 152.4 %while.254 = (s32[]{:T(128)}, f32[384]{0:T(512)S(1)}, f32[384]{0:T(512)}, f32[384,128]{1,0:T(8,128)S(1)}, s32[]{:T(128)}, /*index=5*/bf16[6144,256]{1,0:T(8,128)...) while((s32[]{:T(128)}, f32[384]{0:T(512)S(1)}, ...), condition=%wide.region_59.60_spmd.clone, body=%wide.region_56.59_spmd.clone.sunk | while | flops 25859080 | bytes 1183975 | solution.py:89
  1594.9 169.7 %while.255 = (s32[]{:T(128)}, f32[384]{0:T(512)S(1)}, f32[384]{0:T(512)}, f32[384,128]{1,0:T(8,128)S(1)}, s32[]{:T(128)}, /*index=5*/bf16[6144,256]{1,0:T(8,128)...) while((s32[]{:T(128)}, f32[384]{0:T(512)S(1)}, ...), condition=%wide.region_63.64_spmd.clone, body=%wide.region_60.63_spmd.clone.sunk | while | flops 25859080 | bytes 1183975 | solution.py:89
  1777.3 50.8 %all_to_all.23 = bf16[16,384,128]{2,1,0:T(8,128)(2,1)S(1)} all-to-all(bf16[16,384,128]{2,1,0:T(8,128)(2,1)S(1)} %bitcast.171), channel_id=1, replica_groups=mesh['row'=16,'col'=2] {'row'}, dimensions={0} | all-to-all | bytes 3145728 | tf_op jit(solution)/shard_map/all_to_all | solution.py:92
  1830.5 9.9 all-gather.6.cloned.1.call-done
  1840.4 314.2 %all-gather.8.cloned.1.call-done = bf16[4096,3584]{1,0:T(8,128)(2,1)} async-done(((bf16[256,3584]{1,0:T(8,128)(2,1)}), bf16[4096,3584]{1,0:T(8,128)(2,1)}) %all-gather.8.cloned.1.call-update) | async-done | bytes 29360144 | tf_op jit(solution)/shard_map/all_gather | solution.py:104
  2154.5 19.3 convolution_convert_fusion
  (4173 shorter events, 1541.3 us)
Async XLA Ops:
  6.5 97.1 %all-gather.4.cloned.1.call-start = ((), (), s32[]{:S(2)}) async-start(), calls=%async_computation.3 | async-start | bytes 4456448 | tf_op jit(solution)/shard_map/all_gather | solution.py:23
  7.3 11.0 copy-start.14
  9.9 99.7 %all-to-all-start.1 = ((bf16[16,384,128]{1,2,0:T(8,128)(2,1)}), bf16[16,384,128]{1,2,0:T(8,128)(2,1)S(1)}, u32[]{:S(2)}, u32[]{:S(2)}) async-start(bf16[16,384,128]{1,2,0:T(8,128)(2,1)} %bitcast.4), calls=%async_computation.1 | async-start | bytes 3145728 | tf_op jit(solution)/shard_map/all_to_all | solution.py:33
  110.7 64.9 %all-to-all-start = ((bf16[16,384,256]{2,1,0:T(8,128)(2,1)}), bf16[16,384,256]{2,1,0:T(8,128)(2,1)S(1)}, u32[]{:S(2)}, u32[]{:S(2)}) async-start(bf16[16,384,256]{2,1,0:T(8,128)(2,1)} %bitcast.167), calls=%async_computation | async-start | bytes 6291456 | tf_op jit(solution)/shard_map/all_to_all | solution.py:28
  115.0 1725.4 %all-gather.6.cloned.1.call-start = ((), (), s32[]{:S(2)}) async-start(), calls=%async_computation.4 | async-start | bytes 4718592 | tf_op jit(solution)/shard_map/all_gather | solution.py:100
  247.9 2.5 copy-start.18
  252.4 2.5 copy-start.18
  256.8 2.5 copy-start.18
  261.3 2.5 copy-start.18
  265.7 2.5 copy-start.18
  270.1 2.5 copy-start.18
  279.0 2.5 copy-start.18
  283.4 2.5 copy-start.18
  287.9 2.5 copy-start.18
  296.8 2.5 copy-start.18
  709.4 2.5 copy-start.24
  713.8 2.5 copy-start.24
  718.2 2.5 copy-start.24
  722.6 2.5 copy-start.24
  727.0 2.5 copy-start.24
  731.5 2.5 copy-start.24
  735.9 2.5 copy-start.24
  740.3 2.5 copy-start.24
  744.7 2.5 copy-start.24
  749.2 2.5 copy-start.24
  753.6 2.5 copy-start.24
  758.0 2.5 copy-start.24
  762.4 2.5 copy-start.24
  766.8 2.5 copy-start.24
  771.3 2.5 copy-start.24
  775.7 2.5 copy-start.24
  780.1 2.5 copy-start.24
  784.5 2.5 copy-start.24
  788.9 2.5 copy-start.24
  793.4 2.5 copy-start.24
  797.8 2.5 copy-start.24
  802.2 2.5 copy-start.24
  806.6 2.5 copy-start.24
  811.0 2.5 copy-start.24
  815.5 2.5 copy-start.24
  819.9 2.5 copy-start.24
  824.3 2.5 copy-start.24
  828.7 2.5 copy-start.24
  833.2 2.5 copy-start.24
  837.6 2.5 copy-start.24
  1255.5 2.5 copy-start.28
  1286.5 2.5 copy-start.28
  1290.9 2.5 copy-start.28
  1295.3 2.5 copy-start.28
  1326.3 2.5 copy-start.28
  1330.7 2.5 copy-start.28
  1335.1 2.5 copy-start.28
  1339.6 2.5 copy-start.28
  1764.7 11.0 copy-start.6
  1764.7 11.8 copy-start.7
  1764.7 11.8 copy-start.32
  1764.7 12.0 copy-start.9
  1764.7 12.0 copy-start.33
  1764.7 12.1 copy-start.10
  1764.7 12.1 copy-start.34
  1764.7 12.3 copy-start.12
  1764.7 12.3 copy-start.35
  1764.7 12.4 copy-start.31
  1829.7 324.8 %all-gather.8.cloned.1.call-start = ((), (), s32[]{:S(2)}) async-start(), calls=%async_computation.5 | async-start | bytes 31195136 | tf_op jit(solution)/shard_map/all_gather | solution.py:104
  (369 other events, 908.9 us)
Sparse Core Ops, SparseCore 0:
  10.1 93.4 all-gather.3
  1829.9 10.4 all-gather.5
  1843.1 311.4 all-gather.7
where the time goes:
time: 2210 us; the launch traced here: 2180 us
  matrix products  1010 us (46%)
  other arithmetic  573 us (26%)
  waiting for transfers between devices  444 us (20%)
  blocking collectives  52.9 us (2%)
  local copies, waits for them, and re-layouts  49.7 us (2%)
    dot_general x408, matrix products, key_turn(): jnp.dot(weights.astype(jnp.bfloat16), pairs[:, HEAD:], preferred_element_...  542 us
    add x408, other arithmetic, key_turn(): running_sum = running_sum * rescale + jnp.sum(weights, axis=1)  511 us
    dot_general x408, matrix products, key_turn(): lax.dot_general(query_block, pairs[:, :HEAD], (((1,), (1,)), ((), ())), p...  449 us
    all_gather x1, waiting for transfers between devices, per_device(): lax.all_gather(w_out, 'row', axis=0, tiled=True)  314 us
    all_gather x1, waiting for transfers between devices, per_device(): lax.all_gather(w_kv, 'row', axis=0, tiled=True)  83.3 us
    all_to_all x1, blocking collectives, per_device(): lax.all_to_all(attended.reshape(row_count, stripe, HEAD), 'row', split_ax...  50.8 us

commit v1 on v0

--- a/solution.py
+++ b/solution.py
@@ -1,3 +1,4 @@
+import functools
 import math
 import jax
 import jax.numpy as jnp
@@ -6,6 +7,27 @@
 
 HEAD = 128
 NEG_FILL = -1e30
+
+
+def get_the_shapes(body, row_dim):
+    b_next = jax.lax.psum(1, axis_name="row")
+    main = jax.lax.axis_index("row")
+    tile_out, all_rows, part_next = (b_next, main, body.shape[row_dim])
+    current_block = tuple(
+        (jj * tile_out if j == row_dim else jj for j, jj in enumerate(body.shape))
+    )
+    w_next = jnp.zeros(current_block, body.dtype)
+    f_next = lax.dynamic_update_slice_in_dim(w_next, body, all_rows * part_next, axis=row_dim)
+    for it in range(1, tile_out):
+        f_now = tuple(((j, (j + 1) % tile_out) for j in range(tile_out)))
+        body = jax.lax.ppermute(body, axis_name="row", perm=f_now)
+        f_next = lax.dynamic_update_slice_in_dim(
+            f_next, body, (all_rows - it) % tile_out * part_next, axis=row_dim
+        )
+    return f_next
+
+
+open_the_ladders = functools.partial(get_the_shapes, row_dim=0)
 
 
 def per_device(latent, w_kv, queries, w_out):
@@ -99,11 +121,7 @@
     )
     full_features = lax.all_gather(attn_tokens, "col", axis=1, tiled=True)
     columns = full_features
-    mixed = jnp.dot(
-        columns,
-        lax.all_gather(w_out, "row", axis=0, tiled=True),
-        preferred_element_type=jnp.float32,
-    )
+    mixed = jnp.dot(columns, open_the_ladders(w_out), preferred_element_type=jnp.float32)
     return mixed.astype(jnp.bfloat16)
 
 

time: 2210 us -> 2370 us (1.072)
  the two profiles are of different devices: /device:TPU:0 before, /device:TPU:8 now
where the time goes in v1:
time: 2370 us; the launch traced here: 2340 us
  matrix products  1020 us (43%)
  other arithmetic  582 us (25%)
  waiting for transfers between devices  528 us (22%)
  local copies, waits for them, and re-layouts  100 us (4%)
  starting transfers between devices  75.5 us (3%)
    dot_general x408, matrix products, key_turn(): jnp.dot(weights.astype(jnp.bfloat16), pairs[:, HEAD:], preferred_element_...  550 us
    add x408, other arithmetic, key_turn(): running_sum = running_sum * rescale + jnp.sum(weights, axis=1)  510 us
    ppermute x15, waiting for transfers between devices, get_the_shapes(): body = jax.lax.ppermute(body, axis_name='row', perm=f_now)  454 us
    dot_general x408, matrix products, key_turn(): lax.dot_general(query_block, pairs[:, :HEAD], (((1,), (1,)), ((), ())), p...  449 us
    all_to_all x1, waiting for transfers between devices, per_device(): lax.all_to_all(split_queries, 'row', split_axis=0, concat_axis=1, tiled=T...  63.8 us
    ppermute x15, starting transfers between devices, get_the_shapes(): body = jax.lax.ppermute(body, axis_name='row', perm=f_now)  50.7 us

profile of v1, /device:TPU:8, one launch (start us, length us, event | category | flops | bytes accessed | tf_op | source)
XLA Modules:
  0.0 2344.1 jit_solution(15669312930092674267)
XLA Ops:
  8.8 47.9 %collective-permute-done = bf16[256,3584]{1,0:T(8,128)(2,1)S(1)} collective-permute-done((bf16[256,3584]{1,0:T(8,128)(2,1)}, bf16[256,3584]{1,0:T(8,128)(2,1)S(1)}, u32[]{:S(2)}, u32[]{:S(2)}) %collective-permute-start) | collective-permute-done | bytes 1835040 | tf_op jit(solution)/shard_map/ppermute | solution.py:23
  56.7 70.7 %collective-permute-done.1 = bf16[256,3584]{1,0:T(8,128)(2,1)} collective-permute-done((bf16[256,3584]{1,0:T(8,128)(2,1)S(1)}, bf16[256,3584]{1,0:T(8,128)(2,1)}, u32[]{:S(2)}, u32[]{:S(2)}) %collective-permute-start.1) | collective-permute-done | bytes 1835040 | tf_op jit(solution)/shard_map/ppermute | solution.py:23
  127.4 2.6 copy.44
  130.0 13.7 all-to-all-start.1
  143.6 37.5 %collective-permute-done.2 = bf16[256,3584]{1,0:T(8,128)(2,1)} collective-permute-done((bf16[256,3584]{1,0:T(8,128)(2,1)}, bf16[256,3584]{1,0:T(8,128)(2,1)}, u32[]{:S(2)}, u32[]{:S(2)}) %collective-permute-start.2) | collective-permute-done | bytes 1835040 | tf_op jit(solution)/shard_map/ppermute | solution.py:23
  181.1 2.1 all_gather.9
  183.2 4.0 convolution_convert_fusion.1
  187.2 2.0 copy.64
  189.2 63.8 %all-to-all-done.1 = bf16[16,384,128]{1,2,0:T(8,128)(2,1)S(1)} async-done(((bf16[16,384,128]{1,2,0:T(8,128)(2,1)}), bf16[16,384,128]{1,2,0:T(8,128)(2,1)S(1)}, u32[]{:S(2)}, u32[]{:S(2)}) %all-to-all-start.1) | async-done | bytes 1572896 | tf_op jit(solution)/shard_map/all_to_all | solution.py:55
  254.1 5.4 all-to-all-start
  261.1 94.1 %collective-permute-done.4 = bf16[256,3584]{1,0:T(8,128)(2,1)S(1)} collective-permute-done((bf16[256,3584]{1,0:T(8,128)(2,1)}, bf16[256,3584]{1,0:T(8,128)(2,1)S(1)}, u32[]{:S(2)}, u32[]{:S(2)}) %collective-permute-start.4) | collective-permute-done | bytes 1835040 | tf_op jit(solution)/shard_map/ppermute | solution.py:23
  356.5 43.8 %collective-permute-done.5 = bf16[256,3584]{1,0:T(8,128)(2,1)} collective-permute-done((bf16[256,3584]{1,0:T(8,128)(2,1)S(1)}, bf16[256,3584]{1,0:T(8,128)(2,1)}, u32[]{:S(2)}, u32[]{:S(2)}) %collective-permute-start.5) | collective-permute-done | bytes 1835040 | tf_op jit(solution)/shard_map/ppermute | solution.py:23
  400.3 9.8 broadcast_in_dim.180
  437.2 2.8 constant_dynamic-update-slice_fusion.12
  440.0 4.9 collective-permute-done.6
  444.9 7.3 collective-permute-start.7
  452.8 10.6 while.240
  464.8 26.3 %while.241 = (s32[]{:T(128)}, f32[384]{0:T(512)S(1)}, f32[384]{0:T(512)}, f32[384,128]{1,0:T(8,128)}, s32[]{:T(128)}, /*index=5*/bf16[6144,256]{1,0:T(8,128)(2,1...) while((s32[]{:T(128)}, f32[384]{0:T(512)S(1)}, ...), condition=%wide.region_7.8_spmd.clone, body=%wide.region_4.7_spmd.clone.sunk | while | flops 25859080 | bytes 1183975 | solution.py:111
  491.8 31.6 %while.242 = (s32[]{:T(128)}, f32[384]{0:T(512)S(1)}, f32[384]{0:T(512)}, f32[384,128]{1,0:T(8,128)S(1)}, s32[]{:T(128)}, /*index=5*/bf16[6144,256]{1,0:T(8,128)...) while((s32[]{:T(128)}, f32[384]{0:T(512)S(1)}, ...), condition=%wide.region_11.12_spmd.clone, body=%wide.region_8.11_spmd.clone.sunk | while | flops 25859080 | bytes 1183975 | solution.py:111
  524.7 53.1 %while.243 = (s32[]{:T(128)}, f32[384]{0:T(512)S(1)}, f32[384]{0:T(512)}, f32[384,128]{1,0:T(8,128)}, s32[]{:T(128)}, /*index=5*/bf16[6144,256]{1,0:T(8,128)(2,1...) while((s32[]{:T(128)}, f32[384]{0:T(512)S(1)}, ...), condition=%wide.region_15.16_spmd.clone, body=%wide.region_12.15_spmd.clone.sunk | while | flops 25859080 | bytes 1183975 | solution.py:111
  578.4 53.0 %while.244 = (s32[]{:T(128)}, f32[384]{0:T(512)S(1)}, f32[384]{0:T(512)}, f32[384,128]{1,0:T(8,128)S(1)}, s32[]{:T(128)}, /*index=5*/bf16[6144,256]{1,0:T(8,128)...) while((s32[]{:T(128)}, f32[384]{0:T(512)S(1)}, ...), condition=%wide.region_19.20_spmd.clone, body=%wide.region_16.19_spmd.clone.sunk | while | flops 25859080 | bytes 1183975 | solution.py:111
  632.7 78.0 %while.245 = (s32[]{:T(128)}, f32[384]{0:T(512)S(1)}, f32[384]{0:T(512)}, f32[384,128]{1,0:T(8,128)}, s32[]{:T(128)}, /*index=5*/bf16[6144,256]{1,0:T(8,128)(2,1...) while((s32[]{:T(128)}, f32[384]{0:T(512)S(1)}, ...), condition=%wide.region_23.24_spmd.clone, body=%wide.region_20.23_spmd.clone.sunk | while | flops 25859080 | bytes 1183975 | solution.py:111
  711.3 74.2 %while.246 = (s32[]{:T(128)}, f32[384]{0:T(512)S(1)}, f32[384]{0:T(512)}, f32[384,128]{1,0:T(8,128)S(1)}, s32[]{:T(128)}, /*index=5*/bf16[6144,256]{1,0:T(8,128)...) while((s32[]{:T(128)}, f32[384]{0:T(512)S(1)}, ...), condition=%wide.region_27.28_spmd.clone, body=%wide.region_24.27_spmd.clone.sunk | while | flops 25859080 | bytes 1183975 | solution.py:111
  786.8 105.8 %while.247 = (s32[]{:T(128)}, f32[384]{0:T(512)S(1)}, f32[384]{0:T(512)}, f32[384,128]{1,0:T(8,128)}, s32[]{:T(128)}, /*index=5*/bf16[6144,256]{1,0:T(8,128)(2,1...) while((s32[]{:T(128)}, f32[384]{0:T(512)S(1)}, ...), condition=%wide.region_31.32_spmd.clone, body=%wide.region_28.31_spmd.clone.sunk | while | flops 25859080 | bytes 1183975 | solution.py:111
  893.2 91.9 %while.248 = (s32[]{:T(128)}, f32[384]{0:T(512)S(1)}, f32[384]{0:T(512)}, f32[384,128]{1,0:T(8,128)S(1)}, s32[]{:T(128)}, /*index=5*/bf16[6144,256]{1,0:T(8,128)...) while((s32[]{:T(128)}, f32[384]{0:T(512)S(1)}, ...), condition=%wide.region_35.36_spmd.clone, body=%wide.region_32.35_spmd.clone.sunk | while | flops 25859080 | bytes 1183975 | solution.py:111
  986.5 132.9 %while.249 = (s32[]{:T(128)}, f32[384]{0:T(512)S(1)}, f32[384]{0:T(512)}, f32[384,128]{1,0:T(8,128)}, s32[]{:T(128)}, /*index=5*/bf16[6144,256]{1,0:T(8,128)(2,1...) while((s32[]{:T(128)}, f32[384]{0:T(512)S(1)}, ...), condition=%wide.region_39.40_spmd.clone, body=%wide.region_36.39_spmd.clone.sunk | while | flops 25859080 | bytes 1183975 | solution.py:111
  1120.0 116.6 %while.250 = (s32[]{:T(128)}, f32[384]{0:T(512)S(1)}, f32[384]{0:T(512)}, f32[384,128]{1,0:T(8,128)S(1)}, s32[]{:T(128)}, /*index=5*/bf16[6144,256]{1,0:T(8,128)...) while((s32[]{:T(128)}, f32[384]{0:T(512)S(1)}, ...), condition=%wide.region_43.44_spmd.clone, body=%wide.region_40.43_spmd.clone.sunk | while | flops 25859080 | bytes 1183975 | solution.py:111
  1237.9 159.4 %while.251 = (s32[]{:T(128)}, f32[384]{0:T(512)S(1)}, f32[384]{0:T(512)}, f32[384,128]{1,0:T(8,128)}, s32[]{:T(128)}, /*index=5*/bf16[6144,256]{1,0:T(8,128)(2,1...) while((s32[]{:T(128)}, f32[384]{0:T(512)S(1)}, ...), condition=%wide.region_47.48_spmd.clone, body=%wide.region_44.47_spmd.clone.sunk | while | flops 25859080 | bytes 1183975 | solution.py:111
  1398.0 137.7 %while.252 = (s32[]{:T(128)}, f32[384]{0:T(512)S(1)}, f32[384]{0:T(512)}, f32[384,128]{1,0:T(8,128)S(1)}, s32[]{:T(128)}, /*index=5*/bf16[6144,256]{1,0:T(8,128)...) while((s32[]{:T(128)}, f32[384]{0:T(512)S(1)}, ...), condition=%wide.region_51.52_spmd.clone, body=%wide.region_48.51_spmd.clone.sunk | while | flops 25859080 | bytes 1183975 | solution.py:111
  1536.9 180.7 %while.253 = (s32[]{:T(128)}, f32[384]{0:T(512)S(1)}, f32[384]{0:T(512)}, f32[384,128]{1,0:T(8,128)}, s32[]{:T(128)}, /*index=5*/bf16[6144,256]{1,0:T(8,128)(2,1...) while((s32[]{:T(128)}, f32[384]{0:T(512)S(1)}, ...), condition=%wide.region_55.56_spmd.clone, body=%wide.region_52.55_spmd.clone.sunk | while | flops 25859080 | bytes 1183975 | solution.py:111
  1543.6 1.9 convolution_add_fusion.45
  1547.9 1.9 convolution_add_fusion.45
  1582.3 1.9 convolution_add_fusion.45
  1586.7 1.9 convolution_add_fusion.45
  1591.0 1.9 convolution_add_fusion.45
  1625.4 1.9 convolution_add_fusion.45
  1629.7 1.9 convolution_add_fusion.45
  1664.1 1.9 convolution_add_fusion.45
  1668.4 1.9 convolution_add_fusion.45
  1672.7 1.9 convolution_add_fusion.45
  1707.1 1.9 convolution_add_fusion.45
  1717.7 4.2 collective-permute-start.8
  1722.5 159.3 %while.254 = (s32[]{:T(128)}, f32[384]{0:T(512)S(1)}, f32[384]{0:T(512)}, f32[384,128]{1,0:T(8,128)S(1)}, s32[]{:T(128)}, /*index=5*/bf16[6144,256]{1,0:T(8,128)...) while((s32[]{:T(128)}, f32[384]{0:T(512)S(1)}, ...), condition=%wide.region_59.60_spmd.clone, body=%wide.region_56.59_spmd.clone.sunk | while | flops 25859080 | bytes 1183975 | solution.py:111
  1881.8 36.1 %collective-permute-start.9 = (bf16[256,3584]{1,0:T(8,128)(2,1)}, bf16[256,3584]{1,0:T(8,128)(2,1)}, u32[]{:S(2)}, u32[]{:S(2)}) collective-permute-start(bf16[256,3584]{1,0:T(8,128)(2,1)} %collective-permute-done.8), channel_id=1, source_target_pairs={{0,2},{2,4},{4,6},{6,8},{8,10},{10,12},{12,14},{14,16},{16,18},{18... | collective-permute-start | bytes 5505032 | tf_op jit(solution)/shard_map/ppermute | solution.py:23
  1918.5 170.5 %while.255 = (s32[]{:T(128)}, f32[384]{0:T(512)S(1)}, f32[384]{0:T(512)}, f32[384,128]{1,0:T(8,128)S(1)}, s32[]{:T(128)}, /*index=5*/bf16[6144,256]{1,0:T(8,128)...) while((s32[]{:T(128)}, f32[384]{0:T(512)S(1)}, ...), condition=%wide.region_63.64_spmd.clone, body=%wide.region_60.63_spmd.clone.sunk | while | flops 25859080 | bytes 1183975 | solution.py:111
  2103.0 34.5 %collective-permute-done.10 = bf16[256,3584]{1,0:T(8,128)(2,1)} collective-permute-done((bf16[256,3584]{1,0:T(8,128)(2,1)}, bf16[256,3584]{1,0:T(8,128)(2,1)}, u32[]{:S(2)}, u32[]{:S(2)}) %collective-permute-start.10) | collective-permute-done | bytes 1835040 | tf_op jit(solution)/shard_map/ppermute | solution.py:23
  2146.1 5.7 all-to-all-start.2
  2151.8 37.0 %collective-permute-done.11 = bf16[256,3584]{1,0:T(8,128)(2,1)} collective-permute-done((bf16[256,3584]{1,0:T(8,128)(2,1)}, bf16[256,3584]{1,0:T(8,128)(2,1)}, u32[]{:S(2)}, u32[]{:S(2)}) %collective-permute-start.11) | collective-permute-done | bytes 1835040 | tf_op jit(solution)/shard_map/ppermute | solution.py:23
  2188.9 2.9 constant_dynamic-update-slice_fusion.11
  2191.7 2.8 constant_dynamic-update-slice_fusion.10
  2195.9 2.8 constant_dynamic-update-slice_fusion.8
  2198.8 49.2 %collective-permute-done.12 = bf16[256,3584]{1,0:T(8,128)(2,1)} collective-permute-done((bf16[256,3584]{1,0:T(8,128)(2,1)}, bf16[256,3584]{1,0:T(8,128)(2,1)}, u32[]{:S(2)}, u32[]{:S(2)}) %collective-permute-start.12) | collective-permute-done | bytes 1835040 | tf_op jit(solution)/shard_map/ppermute | solution.py:23
  2248.0 2.8 constant_dynamic-update-slice_fusion.7
  2250.8 2.8 constant_dynamic-update-slice_fusion.6
  2253.7 9.5 all-to-all-done.2
  2264.7 2.9 constant_dynamic-update-slice_fusion.5
  2267.6 2.9 constant_dynamic-update-slice_fusion.4
  2270.5 21.0 collective-permute-done.13
  2291.5 2.9 constant_dynamic-update-slice_fusion.3
  2294.4 2.9 constant_dynamic-update-slice_fusion.2
  2297.3 2.9 constant_dynamic-update-slice_fusion.1
  2300.2 2.9 constant_dynamic-update-slice_fusion
  2303.1 13.7 collective-permute-done.14
  2318.1 19.2 convolution_convert_fusion
  (4230 shorter events, 1615.4 us)
Async XLA Ops:
  6.5 176.7 %all-gather.3.cloned.1.call-start = ((), (), s32[]{:S(2)}) async-start(), calls=%async_computation.3 | async-start | bytes 4456448 | tf_op jit(solution)/shard_map/all_gather | solution.py:45
  7.3 173.9 %copy-start.20 = (bf16[384,256]{1,0:T(8,128)(2,1)S(1)}, bf16[384,256]{1,0:T(8,128)(2,1)}, u32[]{:S(2)}) copy-start(bf16[384,256]{1,0:T(8,128)(2,1)} %param.36) | copy-start | bytes 589828
  7.3 49.4 %collective-permute-start = (bf16[256,3584]{1,0:T(8,128)(2,1)}, bf16[256,3584]{1,0:T(8,128)(2,1)S(1)}, u32[]{:S(2)}, u32[]{:S(2)}) collective-permute-start(bf16[256,3584]{1,0:T(8,128)(2,1)} %param.39), channel_id=1, source_target_pairs={{0,2},{2,4},{4,6},{6,8},{8,10},{10,12},{12,14},{14,16},{16,18},{18... | collective-permute-start | bytes 5505032 | tf_op jit(solution)/shard_map/ppermute | solution.py:23
  56.7 73.3 %copy-start.18 = (bf16[256,3584]{1,0:T(8,128)(2,1)}, bf16[256,3584]{1,0:T(8,128)(2,1)S(1)}, u32[]{:S(2)}) copy-start(bf16[256,3584]{1,0:T(8,128)(2,1)S(1)} %collective-permute-done) | copy-start | bytes 5505028
  56.7 70.7 %collective-permute-start.1 = (bf16[256,3584]{1,0:T(8,128)(2,1)S(1)}, bf16[256,3584]{1,0:T(8,128)(2,1)}, u32[]{:S(2)}, u32[]{:S(2)}) collective-permute-start(bf16[256,3584]{1,0:T(8,128)(2,1)S(1)} %collective-permute-done), channel_id=1, source_target_pairs={{0,2},{2,4},{4,6},{6,8},{8,10},{10,12},{12,14},{14,16},{16,18},{18... | collective-permute-start | bytes 5505032 | tf_op jit(solution)/shard_map/ppermute | solution.py:23
  127.4 53.8 %collective-permute-start.2 = (bf16[256,3584]{1,0:T(8,128)(2,1)}, bf16[256,3584]{1,0:T(8,128)(2,1)}, u32[]{:S(2)}, u32[]{:S(2)}) collective-permute-start(bf16[256,3584]{1,0:T(8,128)(2,1)} %collective-permute-done.1), channel_id=1, source_target_pairs={{0,2},{2,4},{4,6},{6,8},{8,10},{10,12},{12,14},{14,16},{16,18},{18... | collective-permute-start | bytes 5505032 | tf_op jit(solution)/shard_map/ppermute | solution.py:23
  130.0 123.0 %all-to-all-start.1 = ((bf16[16,384,128]{1,2,0:T(8,128)(2,1)}), bf16[16,384,128]{1,2,0:T(8,128)(2,1)S(1)}, u32[]{:S(2)}, u32[]{:S(2)}) async-start(bf16[16,384,128]{1,2,0:T(8,128)(2,1)} %bitcast.4), calls=%async_computation.1 | async-start | bytes 3145728 | tf_op jit(solution)/shard_map/all_to_all | solution.py:55
  181.1 78.4 %collective-permute-start.3 = (bf16[256,3584]{1,0:T(8,128)(2,1)}, bf16[256,3584]{1,0:T(8,128)(2,1)}, u32[]{:S(2)}, u32[]{:S(2)}) collective-permute-start(bf16[256,3584]{1,0:T(8,128)(2,1)} %collective-permute-done.2), channel_id=1, source_target_pairs={{0,2},{2,4},{4,6},{6,8},{8,10},{10,12},{12,14},{14,16},{16,18},{18... | collective-permute-start | bytes 5505032 | tf_op jit(solution)/shard_map/ppermute | solution.py:23
  254.1 198.1 %all-to-all-start = ((bf16[16,384,256]{2,1,0:T(8,128)(2,1)}), bf16[16,384,256]{2,1,0:T(8,128)(2,1)S(1)}, u32[]{:S(2)}, u32[]{:S(2)}) async-start(bf16[16,384,256]{2,1,0:T(8,128)(2,1)} %bitcast.167), calls=%async_computation | async-start | bytes 6291456 | tf_op jit(solution)/shard_map/all_to_all | solution.py:50
  259.5 95.6 %collective-permute-start.4 = (bf16[256,3584]{1,0:T(8,128)(2,1)}, bf16[256,3584]{1,0:T(8,128)(2,1)S(1)}, u32[]{:S(2)}, u32[]{:S(2)}) collective-permute-start(bf16[256,3584]{1,0:T(8,128)(2,1)} %collective-permute-done.3), channel_id=1, source_target_pairs={{0,2},{2,4},{4,6},{6,8},{8,10},{10,12},{12,14},{14,16},{16,18},{18... | collective-permute-start | bytes 5505032 | tf_op jit(solution)/shard_map/ppermute | solution.py:23
  356.5 43.8 %collective-permute-start.5 = (bf16[256,3584]{1,0:T(8,128)(2,1)S(1)}, bf16[256,3584]{1,0:T(8,128)(2,1)}, u32[]{:S(2)}, u32[]{:S(2)}) collective-permute-start(bf16[256,3584]{1,0:T(8,128)(2,1)S(1)} %collective-permute-done.4), channel_id=1, source_target_pairs={{0,2},{2,4},{4,6},{6,8},{8,10},{10,12},{12,14},{14,16},{16,18},{18... | collective-permute-start | bytes 5505032 | tf_op jit(solution)/shard_map/ppermute | solution.py:23
  400.3 44.7 %collective-permute-start.6 = (bf16[256,3584]{1,0:T(8,128)(2,1)}, bf16[256,3584]{1,0:T(8,128)(2,1)}, u32[]{:S(2)}, u32[]{:S(2)}) collective-permute-start(bf16[256,3584]{1,0:T(8,128)(2,1)} %collective-permute-done.5), channel_id=1, source_target_pairs={{0,2},{2,4},{4,6},{6,8},{8,10},{10,12},{12,14},{14,16},{16,18},{18... | collective-permute-start | bytes 5505032 | tf_op jit(solution)/shard_map/ppermute | solution.py:23
  400.3 9.8 copy-start.15
  410.1 3.5 copy-start.14
  444.9 1272.7 %collective-permute-start.7 = (bf16[256,3584]{1,0:T(8,128)(2,1)}, bf16[256,3584]{1,0:T(8,128)(2,1)}, u32[]{:S(2)}, u32[]{:S(2)}) collective-permute-start(bf16[256,3584]{1,0:T(8,128)(2,1)} %collective-permute-done.6), channel_id=1, source_target_pairs={{0,2},{2,4},{4,6},{6,8},{8,10},{10,12},{12,14},{14,16},{16,18},{18... | collective-permute-start | bytes 5505032 | tf_op jit(solution)/shard_map/ppermute | solution.py:23
  1717.7 164.1 %collective-permute-start.8 = (bf16[256,3584]{1,0:T(8,128)(2,1)}, bf16[256,3584]{1,0:T(8,128)(2,1)}, u32[]{:S(2)}, u32[]{:S(2)}) collective-permute-start(bf16[256,3584]{1,0:T(8,128)(2,1)} %collective-permute-done.7), channel_id=1, source_target_pairs={{0,2},{2,4},{4,6},{6,8},{8,10},{10,12},{12,14},{14,16},{16,18},{18... | collective-permute-start | bytes 5505032 | tf_op jit(solution)/shard_map/ppermute | solution.py:23
  1881.8 36.8 %copy-start.11 = (f32[384,128]{1,0:T(8,128)}, f32[384,128]{1,0:T(8,128)S(1)}, u32[]{:S(2)}) copy-start(f32[384,128]{1,0:T(8,128)S(1)} %get-tuple-element.737) | copy-start | bytes 589828
  1881.8 207.3 %collective-permute-start.9 = (bf16[256,3584]{1,0:T(8,128)(2,1)}, bf16[256,3584]{1,0:T(8,128)(2,1)}, u32[]{:S(2)}, u32[]{:S(2)}) collective-permute-start(bf16[256,3584]{1,0:T(8,128)(2,1)} %collective-permute-done.8), channel_id=1, source_target_pairs={{0,2},{2,4},{4,6},{6,8},{8,10},{10,12},{12,14},{14,16},{16,18},{18... | collective-permute-start | bytes 5505032 | tf_op jit(solution)/shard_map/ppermute | solution.py:23
  1922.1 2.5 copy-start.36
  1925.6 2.5 copy-start.36
  1943.4 2.5 copy-start.36
  1946.9 2.5 copy-start.36
  1950.5 2.5 copy-start.36
  1954.0 2.5 copy-start.36
  1957.6 2.5 copy-start.36
  1971.8 2.5 copy-start.36
  1975.4 2.5 copy-start.36
  1978.9 2.5 copy-start.36
  1982.5 2.5 copy-start.36
  1986.0 2.5 copy-start.36
  1989.6 2.5 copy-start.36
  2003.8 2.5 copy-start.36
  2007.3 2.5 copy-start.36
  2010.9 2.5 copy-start.36
  2014.4 2.5 copy-start.36
  2018.0 2.5 copy-start.36
  2021.5 2.5 copy-start.36
  2035.8 2.5 copy-start.36
  2039.3 2.5 copy-start.36
  2042.9 2.5 copy-start.36
  2046.4 2.5 copy-start.36
  2053.5 2.5 copy-start.36
  2071.3 2.5 copy-start.36
  2074.8 2.5 copy-start.36
  2078.4 2.5 copy-start.36
  2085.5 2.5 copy-start.36
  2089.0 51.8 %copy-start.6 = (f32[384,128]{1,0:T(8,128)S(1)}, f32[384,128]{1,0:T(8,128)}, u32[]{:S(2)}) copy-start(f32[384,128]{1,0:T(8,128)} %copy-done.5) | copy-start | bytes 589828
  2089.0 53.2 %copy-start.7 = (f32[384,128]{1,0:T(8,128)S(1)}, f32[384,128]{1,0:T(8,128)}, u32[]{:S(2)}) copy-start(f32[384,128]{1,0:T(8,128)} %get-tuple-element.731) | copy-start | bytes 589828
  2089.0 53.2 %copy-start.38 = (f32[384]{0:T(512)S(1)}, f32[384]{0:T(512)}, u32[]{:S(2)}) copy-start(f32[384]{0:T(512)} %get-tuple-element.732) | copy-start | bytes 4612
  2089.1 54.0 %copy-start.9 = (f32[384,128]{1,0:T(8,128)S(1)}, f32[384,128]{1,0:T(8,128)}, u32[]{:S(2)}) copy-start(f32[384,128]{1,0:T(8,128)} %copy-done.8) | copy-start | bytes 589828
  2089.1 54.0 %copy-start.39 = (f32[384]{0:T(512)S(1)}, f32[384]{0:T(512)}, u32[]{:S(2)}) copy-start(f32[384]{0:T(512)} %get-tuple-element.734) | copy-start | bytes 4612
  2089.1 54.7 %copy-start.10 = (f32[384,128]{1,0:T(8,128)S(1)}, f32[384,128]{1,0:T(8,128)}, u32[]{:S(2)}) copy-start(f32[384,128]{1,0:T(8,128)} %get-tuple-element.735) | copy-start | bytes 589828
  2089.1 54.7 %copy-start.40 = (f32[384]{0:T(512)S(1)}, f32[384]{0:T(512)}, u32[]{:S(2)}) copy-start(f32[384]{0:T(512)} %get-tuple-element.736) | copy-start | bytes 4612
  2089.1 55.5 %copy-start.12 = (f32[384,128]{1,0:T(8,128)S(1)}, f32[384,128]{1,0:T(8,128)}, u32[]{:S(2)}) copy-start(f32[384,128]{1,0:T(8,128)} %copy-done.11) | copy-start | bytes 589828
  2089.1 55.5 %copy-start.41 = (f32[384]{0:T(512)S(1)}, f32[384]{0:T(512)}, u32[]{:S(2)}) copy-start(f32[384]{0:T(512)} %get-tuple-element.738) | copy-start | bytes 4612
  2089.1 56.2 %copy-start.37 = (f32[384]{0:T(512)S(1)}, f32[384]{0:T(512)}, u32[]{:S(2)}) copy-start(f32[384]{0:T(512)} %get-tuple-element.740) | copy-start | bytes 4612
  2089.1 48.3 %collective-permute-start.10 = (bf16[256,3584]{1,0:T(8,128)(2,1)}, bf16[256,3584]{1,0:T(8,128)(2,1)}, u32[]{:S(2)}, u32[]{:S(2)}) collective-permute-start(bf16[256,3584]{1,0:T(8,128)(2,1)} %collective-permute-done.9), channel_id=1, source_target_pairs={{0,2},{2,4},{4,6},{6,8},{8,10},{10,12},{12,14},{14,16},{16,18},{18... | collective-permute-start | bytes 5505032 | tf_op jit(solution)/shard_map/ppermute | solution.py:23
  2137.4 51.4 %collective-permute-start.11 = (bf16[256,3584]{1,0:T(8,128)(2,1)}, bf16[256,3584]{1,0:T(8,128)(2,1)}, u32[]{:S(2)}, u32[]{:S(2)}) collective-permute-start(bf16[256,3584]{1,0:T(8,128)(2,1)} %collective-permute-done.10), channel_id=1, source_target_pairs={{0,2},{2,4},{4,6},{6,8},{8,10},{10,12},{12,14},{14,16},{16,18},{18... | collective-permute-start | bytes 5505032 | tf_op jit(solution)/shard_map/ppermute | solution.py:23
  2146.1 117.0 %all-to-all-start.2 = ((bf16[16,384,128]{2,1,0:T(8,128)(2,1)}), bf16[16,384,128]{2,1,0:T(8,128)(2,1)S(1)}, u32[]{:S(2)}, u32[]{:S(2)}) async-start(bf16[16,384,128]{2,1,0:T(8,128)(2,1)} %bitcast.21), calls=%async_computation.2 | async-start | bytes 3145728 | tf_op jit(solution)/shard_map/all_to_all | solution.py:114
  2151.8 166.3 %all-gather.5.cloned.1.call-start = ((), (), s32[]{:S(2)}) async-start(), calls=%async_computation.4 | async-start | bytes 4718592 | tf_op jit(solution)/shard_map/all_gather | solution.py:122
  2151.8 42.8 %copy-start.17 = (bf16[256,3584]{1,0:T(8,128)(2,1)S(1)}, bf16[256,3584]{1,0:T(8,128)(2,1)}, u32[]{:S(2)}) copy-start(bf16[256,3584]{1,0:T(8,128)(2,1)} %copy-done.16) | copy-start | bytes 5505028
  2188.9 59.1 %collective-permute-start.12 = (bf16[256,3584]{1,0:T(8,128)(2,1)}, bf16[256,3584]{1,0:T(8,128)(2,1)}, u32[]{:S(2)}, u32[]{:S(2)}) collective-permute-start(bf16[256,3584]{1,0:T(8,128)(2,1)} %collective-permute-done.11), channel_id=1, source_target_pairs={{0,2},{2,4},{4,6},{6,8},{8,10},{10,12},{12,14},{14,16},{16,18},{18... | collective-permute-start | bytes 5505032 | tf_op jit(solution)/shard_map/ppermute | solution.py:23
  2248.0 43.5 %collective-permute-start.13 = (bf16[256,3584]{1,0:T(8,128)(2,1)}, bf16[256,3584]{1,0:T(8,128)(2,1)}, u32[]{:S(2)}, u32[]{:S(2)}) collective-permute-start(bf16[256,3584]{1,0:T(8,128)(2,1)} %collective-permute-done.12), channel_id=1, source_target_pairs={{0,2},{2,4},{4,6},{6,8},{8,10},{10,12},{12,14},{14,16},{16,18},{18... | collective-permute-start | bytes 5505032 | tf_op jit(solution)/shard_map/ppermute | solution.py:23
  2291.5 25.2 %collective-permute-start.14 = (bf16[256,3584]{1,0:T(8,128)(2,1)}, bf16[256,3584]{1,0:T(8,128)(2,1)S(1)}, u32[]{:S(2)}, u32[]{:S(2)}) collective-permute-start(bf16[256,3584]{1,0:T(8,128)(2,1)} %collective-permute-done.13), channel_id=1, source_target_pairs={{0,2},{2,4},{4,6},{6,8},{8,10},{10,12},{12,14},{14,16},{16,18},{18... | collective-permute-start | bytes 5505032 | tf_op jit(solution)/shard_map/ppermute | solution.py:23
  (390 other events, 961.7 us)
Sparse Core Ops, SparseCore 0:
  10.1 128.2 all-gather.2
  2264.9 11.7 all-gather.4
